TPU v7x, 256 devices: a whole 4x4x8 slice. The times are simulated.
256 devices in a mesh: leaf: 16 (over x, y), rows: 16 (over z, core).
Axes of the slice: x: 4, y: 4, z: 8, core: 2. Of those that a mesh axis runs over, the one named last changes fastest.
Arguments:
- rhs_top: float32 [1, 4096, 128], P(None, 'rows'), may hold values from -6 to 6
- rhs_one: float32 [2, 2048, 128], P(None, 'rows'), may hold values from -6 to 6
- rhs_two: float32 [4, 2048, 128], P(None, 'rows'), may hold values from -6 to 6
- rhs_three: float32 [8, 1024, 128], P(None, 'rows'), may hold values from -6 to 6
- inv_top: float32 [4096, 4096], P('rows', 'leaf')
- inv_one: float32 [2048, 4096], P('rows', 'leaf')
- inv_two: float32 [2048, 8192], P('rows', 'leaf')
- inv_three: float32 [1024, 8192], P('rows', 'leaf')
- panel_one: float32 [4096, 2048], P('leaf', 'rows'), may hold values from -0.0625 to 0.0625
- panel_two: float32 [8192, 4096], P('leaf', 'rows'), may hold values from -0.0625 to 0.0625
- panel_three: float32 [8192, 4096], P('leaf', 'rows'), may hold values from -0.09375 to 0.09375
- rows_one: int32 [2, 16], P(None, 'rows'), may hold values from 0 to 31, as said below
- rows_two: int32 [4, 32], P(None, 'rows'), may hold values from 0 to 47, as said below
- rows_three: int32 [8, 32], P(None, 'rows'), may hold values from 0 to 63, as said below
Outputs:
- solution_top: float32 [1, 4096, 128], P(None, 'rows')
- solution_one: float32 [2, 2048, 128], P(None, 'rows')
- solution_two: float32 [4, 2048, 128], P(None, 'rows')
- solution_three: float32 [8, 1024, 128], P(None, 'rows')
Inputs may be any that keep to these rules, and one draw needn't show every extreme that they name: `rows_one`: each row lists 16 different blocks of a chain of 32 blocks, the chain's first and last among them. `rows_two`: each row lists 32 different blocks of a chain of 48 blocks, the chain's first and last among them. `rows_three`: each row lists 32 different blocks of a chain of 64 blocks, the chain's first and last among them.
All inputs are finite; a program needn't handle non-finite values.
Results may differ from a plain program's by a relative error of at most 0.0001.
Values sent between devices are 32-bit elements; how exact they have to be, the bound alone decides.
A program may use at most 64 MiB of HBM per device.

v0:
```python
import jax
import jax.numpy as jnp
from jax import lax
from jax.sharding import PartitionSpec as P

SEP0 = 4096
SEP1 = 2048
SEP2 = 2048
SEP3 = 1024
BLOCK = 128


def layout(sep_count, sep_size):
    span_rows = sep_count * sep_size // lax.axis_size("leaf")
    held_count = max(1, span_rows // sep_size)
    part_rows = min(span_rows, sep_size)
    first_sep = lax.axis_index("leaf") * span_rows // sep_size
    return (held_count, part_rows, first_sep)


def forward_solve(inverse, source, sep_count, sep_size):
    held_count, part_rows, first_sep = layout(sep_count, sep_size)
    picked = lax.dynamic_slice_in_dim(source, first_sep, held_count, 0)
    blocks = inverse.reshape(inverse.shape[0], held_count, part_rows)
    partial_y = jnp.einsum("csr,scn->srn", blocks, picked, precision=lax.Precision.HIGHEST)
    return lax.psum(partial_y, "rows")


def chain_matches(index_rows, first_sep, held_count, chain_count, listed):
    picked_rows = lax.dynamic_slice_in_dim(index_rows, first_sep, held_count, 0)
    column_ids = lax.broadcasted_iota(jnp.int32, (held_count, chain_count, listed), 1)
    return (column_ids == picked_rows[:, None, :]).astype(jnp.float32)


def ancestor_terms(panel, index_rows, solved_rows, sep_sizes, sep_counts, level_at):
    held_count, part_rows, first_sep = layout(sep_counts[level_at], sep_sizes[level_at])
    width_rhs = solved_rows.shape[2]
    listed = panel.shape[1] // BLOCK
    chain_count = sum(sep_sizes[:level_at]) // BLOCK
    panel_cut = panel.reshape(held_count, part_rows, listed * BLOCK)
    updates = jnp.einsum("sra,srn->san", panel_cut, solved_rows, precision=lax.Precision.HIGHEST)
    matches = chain_matches(index_rows, first_sep, held_count, chain_count, listed)
    spread = jnp.einsum(
        "sck,skbn->scbn",
        matches,
        updates.reshape(held_count, listed, BLOCK, width_rhs),
        precision=lax.Precision.HIGHEST,
    )
    owners = first_sep + jnp.arange(held_count, dtype=jnp.int32)
    results = []
    offset = 0
    for upper in range(level_at):
        blocks_up = sep_sizes[upper] // BLOCK
        segment = spread[:, offset : offset + blocks_up].reshape(
            held_count, sep_sizes[upper], width_rhs
        )
        target_ids = lax.broadcasted_iota(jnp.int32, (held_count, sep_counts[upper]), 1)
        target = (target_ids == (owners >> level_at - upper)[:, None]).astype(jnp.float32)
        results.append(jnp.einsum("sq,srn->qrn", target, segment, precision=lax.Precision.HIGHEST))
        offset = offset + blocks_up
    return results


def reduce_dense(parts):
    column_parts = lax.psum_scatter(parts, "rows", scatter_dimension=1, tiled=True)
    return lax.psum(column_parts, "leaf")


def backward_panel(panel, index_rows, gathered, solved_rows, sep_sizes, sep_counts, level_at):
    held_count, part_rows, first_sep = layout(sep_counts[level_at], sep_sizes[level_at])
    width_rhs = solved_rows.shape[2]
    listed = panel.shape[1] // BLOCK
    chain_count = sum(sep_sizes[:level_at]) // BLOCK
    owners = first_sep + jnp.arange(held_count, dtype=jnp.int32)
    pieces = []
    for upper in range(level_at):
        target_ids = lax.broadcasted_iota(jnp.int32, (held_count, sep_counts[upper]), 1)
        target = (target_ids == (owners >> level_at - upper)[:, None]).astype(jnp.float32)
        pieces.append(
            jnp.einsum("sq,qrn->srn", target, gathered[upper], precision=lax.Precision.HIGHEST)
        )
    chain_x = jnp.concatenate(pieces, axis=1).reshape(held_count, chain_count, BLOCK, width_rhs)
    matches = chain_matches(index_rows, first_sep, held_count, chain_count, listed)
    chosen = jnp.einsum("sck,scbn->skbn", matches, chain_x, precision=lax.Precision.HIGHEST)
    panel_cut = panel.reshape(held_count, part_rows, listed * BLOCK)
    partial_g = jnp.einsum(
        "sra,san->srn",
        panel_cut,
        chosen.reshape(held_count, listed * BLOCK, width_rhs),
        precision=lax.Precision.HIGHEST,
    )
    return solved_rows - lax.psum(partial_g, "rows")


def backward_solve(inverse, residue, sep_count, sep_size):
    held_count, part_rows, first_sep = layout(sep_count, sep_size)
    blocks = inverse.reshape(inverse.shape[0], held_count, part_rows)
    partial_x = jnp.einsum("csr,srn->scn", blocks, residue, precision=lax.Precision.HIGHEST)
    owners = first_sep + jnp.arange(held_count, dtype=jnp.int32)
    place_ids = lax.broadcasted_iota(jnp.int32, (held_count, sep_count), 1)
    placing = (place_ids == owners[:, None]).astype(jnp.float32)
    dense = jnp.einsum("sq,scn->qcn", placing, partial_x, precision=lax.Precision.HIGHEST)
    return lax.psum(dense, "leaf")


def body(
    rhs_top,
    rhs_one,
    rhs_two,
    rhs_three,
    inv_top,
    inv_one,
    inv_two,
    inv_three,
    panel_one,
    panel_two,
    panel_three,
    rows_one,
    rows_two,
    rows_three,
):
    sep_sizes = [SEP0, SEP1, SEP2, SEP3]
    sep_counts = [1, 2, 4, 8]
    right_sides = [rhs_top, rhs_one, rhs_two, rhs_three]
    inverses = [inv_top, inv_one, inv_two, inv_three]
    panels = [None, panel_one, panel_two, panel_three]
    indices = [None, rows_one, rows_two, rows_three]
    solved = [None, None, None, None]
    owed_rows = [jnp.zeros(item.shape, jnp.float32) for item in right_sides]
    for level_at in (3, 2, 1, 0):
        source = right_sides[level_at] - owed_rows[level_at]
        solved[level_at] = forward_solve(
            inverses[level_at], source, sep_counts[level_at], sep_sizes[level_at]
        )
        if level_at > 0:
            fresh = ancestor_terms(
                panels[level_at],
                indices[level_at],
                solved[level_at],
                sep_sizes,
                sep_counts,
                level_at,
            )
            reduced = reduce_dense(tuple(fresh))
            for upper in range(level_at):
                owed_rows[upper] = owed_rows[upper] + reduced[upper]
    gathered = []
    results = []
    for level_at in range(4):
        residue = solved[level_at]
        if level_at > 0:
            residue = backward_panel(
                panels[level_at],
                indices[level_at],
                gathered,
                solved[level_at],
                sep_sizes,
                sep_counts,
                level_at,
            )
        solution_cols = backward_solve(
            inverses[level_at], residue, sep_counts[level_at], sep_sizes[level_at]
        )
        results.append(solution_cols)
        if level_at < 3:
            gathered.append(lax.all_gather(solution_cols, "rows", axis=1, tiled=True))
    return (results[0], results[1], results[2], results[3])


def solution(mesh):
    return jax.shard_map(
        body,
        mesh=mesh,
        in_specs=(
            P(None, "rows", None),
            P(None, "rows", None),
            P(None, "rows", None),
            P(None, "rows", None),
            P("rows", "leaf"),
            P("rows", "leaf"),
            P("rows", "leaf"),
            P("rows", "leaf"),
            P("leaf", "rows"),
            P("leaf", "rows"),
            P("leaf", "rows"),
            P(None, "rows"),
            P(None, "rows"),
            P(None, "rows"),
        ),
        out_specs=(
            P(None, "rows", None),
            P(None, "rows", None),
            P(None, "rows", None),
            P(None, "rows", None),
        ),
        check_vma=False,
    )
```

profile of v0, /device:TPU:2, one launch (start us, length us, event | category | flops | bytes accessed | tf_op | source)
XLA Modules:
  0.0 1859.5 jit_solution(8080732922114036708)
XLA Ops:
  7.2 2.1 convolution_bitcast_fusion.5
  9.4 0.9 fusion.41
  10.3 113.3 %all-reduce.15.cloned.1.call-done = f32[1,512,128]{1,2,0:T(8,128)} async-done(((f32[1,512,128]{1,2,0:T(8,128)}), f32[1,512,128]{1,2,0:T(8,128)}) %all-reduce.15.cloned.1.call-update) | async-done | bytes 262160 | tf_op jit(solution)/shard_map/psum | solution.py:26
  123.6 1.5 convolution_bitcast_fusion.8
  125.4 1.9 convolution_bitcast_fusion
  127.5 1.8 copy-done.1
  129.6 2.3 broadcast_multiply_fusion
  132.0 63.9 %reduce-scatter.4.cloned.1.call-done = f32[4,128,128]{2,1,0:T(8,128)} async-done(((f32[4,2048,128]{2,1,0:T(8,128)}), f32[4,128,128]{2,1,0:T(8,128)}) %reduce-scatter.4.cloned.1.call-update) | async-done | bytes 262160 | tf_op jit(solution)/shard_map/reduce_scatter | solution.py:65
  196.0 96.3 %all-reduce.17.cloned.1.call-done = f32[4,128,128]{2,1,0:T(8,128)} async-done(((f32[4,128,128]{2,1,0:T(8,128)}), f32[4,128,128]{2,1,0:T(8,128)}) %all-reduce.17.cloned.1.call-update) | async-done | bytes 262160 | tf_op jit(solution)/shard_map/psum | solution.py:66
  292.3 2.0 convolution_bitcast_fusion.4
  294.9 109.9 %all-reduce.19.cloned.1.call-done = f32[1,512,128]{1,2,0:T(8,128)} async-done(((f32[1,512,128]{1,2,0:T(8,128)}), f32[1,512,128]{1,2,0:T(8,128)}) %all-reduce.19.cloned.1.call-update) | async-done | bytes 262160 | tf_op jit(solution)/shard_map/psum | solution.py:26
  404.8 1.3 convolution_bitcast_fusion.7
  406.4 1.5 convolution_bitcast_fusion.1
  408.3 1.2 copy-done.2
  409.6 1.7 multiply_add_fusion
  411.4 60.6 %reduce-scatter.6.cloned.1.call-done = f32[2,128,128]{2,1,0:T(8,128)} async-done(((f32[2,2048,128]{2,1,0:T(8,128)}), f32[2,128,128]{2,1,0:T(8,128)}) %reduce-scatter.6.cloned.1.call-update) | async-done | bytes 131088 | tf_op jit(solution)/shard_map/reduce_scatter | solution.py:65
  473.3 93.1 %all-reduce.39.cloned.1.call-done = f32[2,128,128]{2,1,0:T(8,128)} async-done(((f32[2,128,128]{2,1,0:T(8,128)}), f32[2,128,128]{2,1,0:T(8,128)}) %all-reduce.39.cloned.1.call-update) | async-done | bytes 131088 | tf_op jit(solution)/shard_map/psum | solution.py:66
  566.4 1.8 convolution_bitcast_fusion.10
  568.3 2.8 fusion.2
  571.0 1.2 copy.29
  572.3 106.2 %all-reduce.21.cloned.1.call-done = f32[1,256,128]{1,2,0:T(8,128)} async-done(((f32[1,256,128]{1,2,0:T(8,128)}), f32[1,256,128]{1,2,0:T(8,128)}) %all-reduce.21.cloned.1.call-update) | async-done | bytes 131088 | tf_op jit(solution)/shard_map/psum | solution.py:26
  678.5 1.2 convolution_bitcast_fusion.12
  680.0 1.6 bitcast_add_fusion
  681.7 60.9 %reduce-scatter.8.cloned.1.call-done = f32[1,256,128]{2,1,0:T(8,128)} async-done(((f32[1,4096,128]{2,1,0:T(8,128)}), f32[1,256,128]{2,1,0:T(8,128)}) %reduce-scatter.8.cloned.1.call-update) | async-done | bytes 131088 | tf_op jit(solution)/shard_map/reduce_scatter | solution.py:65
  742.6 94.3 %all-reduce.41.cloned.1.call-done = f32[1,256,128]{2,1,0:T(8,128)} async-done(((f32[1,256,128]{2,1,0:T(8,128)}), f32[1,256,128]{2,1,0:T(8,128)}) %all-reduce.41.cloned.1.call-update) | async-done | bytes 131088 | tf_op jit(solution)/shard_map/psum | solution.py:66
  837.0 2.0 convolution_bitcast_fusion.6
  839.0 109.9 %all-reduce.23.cloned.1.call-done = f32[256,128]{0,1:T(8,128)} async-done(((f32[256,128]{0,1:T(8,128)}), f32[256,128]{0,1:T(8,128)}) %all-reduce.23.cloned.1.call-update) | async-done | bytes 131088 | tf_op jit(solution)/shard_map/psum | solution.py:26
  948.9 2.0 fusion.7
  951.0 95.2 %all-reduce.25.cloned.1.call-done = f32[1,256,128]{1,2,0:T(8,128)} async-done(((f32[1,256,128]{1,2,0:T(8,128)}), f32[1,256,128]{1,2,0:T(8,128)}) %all-reduce.25.cloned.1.call-update) | async-done | bytes 131088 | tf_op jit(solution)/shard_map/psum | solution.py:103
  1046.4 40.7 %all-gather.4.cloned.1.call-done = f32[1,4096,128]{1,2,0:T(8,128)} async-done(((f32[1,256,128]{1,2,0:T(8,128)}), f32[1,4096,128]{1,2,0:T(8,128)}) %all-gather.4.cloned.1.call-update) | async-done | bytes 2097168 | tf_op jit(solution)/shard_map/all_gather | solution.py:166
  1087.2 3.7 broadcast_multiply_fusion.1
  1091.3 1.5 fusion.31
  1092.7 0.9 convolution_bitcast_fusion.9
  1093.8 107.9 %all-reduce.27.cloned.1.call-done = f32[1,256,128]{1,2,0:T(8,128)} async-done(((f32[1,256,128]{1,2,0:T(8,128)}), f32[1,256,128]{1,2,0:T(8,128)}) %all-reduce.27.cloned.1.call-update) | async-done | bytes 131088 | tf_op jit(solution)/shard_map/psum | solution.py:92
  1201.6 1.2 convolution_bitcast_fusion.11
  1203.7 95.0 %all-reduce.29.cloned.1.call-done = f32[2,128,128]{2,1,0:T(8,128)} async-done(((f32[2,128,128]{2,1,0:T(8,128)}), f32[2,128,128]{2,1,0:T(8,128)}) %all-reduce.29.cloned.1.call-update) | async-done | bytes 131088 | tf_op jit(solution)/shard_map/psum | solution.py:103
  1298.8 40.9 %all-gather.6.cloned.1.call-done = f32[2,2048,128]{2,1,0:T(8,128)} async-done(((f32[2,128,128]{2,1,0:T(8,128)}), f32[2,2048,128]{2,1,0:T(8,128)}) %all-gather.6.cloned.1.call-update) | async-done | bytes 2097168 | tf_op jit(solution)/shard_map/all_gather | solution.py:166
  1339.7 7.6 fusion.5
  1347.3 3.6 copy.42
  1350.9 1.5 maximum_bitcast_fusion.1
  1352.4 2.2 copy.47
  1354.5 3.6 copy.34
  1358.1 3.0 fusion.33
  1361.2 1.4 convolution_bitcast_fusion.3
  1362.7 108.2 %all-reduce.31.cloned.1.call-done = f32[1,512,128]{1,2,0:T(8,128)} async-done(((f32[1,512,128]{1,2,0:T(8,128)}), f32[1,512,128]{1,2,0:T(8,128)}) %all-reduce.31.cloned.1.call-update) | async-done | bytes 262160 | tf_op jit(solution)/shard_map/psum | solution.py:92
  1470.9 1.3 convolution_bitcast_fusion.13
  1472.3 0.8 broadcast_multiply_fusion.4
  1473.2 96.5 %all-reduce.33.cloned.1.call-done = f32[4,128,128]{2,1,0:T(8,128)} async-done(((f32[4,128,128]{2,1,0:T(8,128)}), f32[4,128,128]{2,1,0:T(8,128)}) %all-reduce.33.cloned.1.call-update) | async-done | bytes 262160 | tf_op jit(solution)/shard_map/psum | solution.py:103
  1570.0 6.6 fusion.3
  1576.6 1.9 copy.43
  1578.5 34.7 %all-gather.8.cloned.1.call-done = f32[4,2048,128]{2,1,0:T(8,128)} async-done(((f32[4,128,128]{2,1,0:T(8,128)}), f32[4,2048,128]{2,1,0:T(8,128)}) %all-gather.8.cloned.1.call-update) | async-done | bytes 4194320 | tf_op jit(solution)/shard_map/all_gather | solution.py:166
  1613.1 9.6 fusion
  1622.7 3.8 copy.45
  1626.6 1.9 maximum_bitcast_fusion
  1628.4 2.7 copy.48
  1631.1 5.5 copy.37
  1636.6 3.7 fusion.36
  1640.4 1.4 convolution_bitcast_fusion.2
  1641.9 108.6 %all-reduce.35.cloned.1.call-done = f32[1,512,128]{1,2,0:T(8,128)} async-done(((f32[1,512,128]{1,2,0:T(8,128)}), f32[1,512,128]{1,2,0:T(8,128)}) %all-reduce.35.cloned.1.call-update) | async-done | bytes 262160 | tf_op jit(solution)/shard_map/psum | solution.py:92
  1750.5 1.3 convolution_bitcast_fusion.14
  1751.8 0.8 broadcast_multiply_fusion.3
  1752.7 0.8 copy.39
  1753.4 95.9 %all-reduce.37.cloned.1.call-done = f32[8,64,128]{2,1,0:T(8,128)} async-done(((f32[8,64,128]{2,1,0:T(8,128)}), f32[8,64,128]{2,1,0:T(8,128)}) %all-reduce.37.cloned.1.call-update) | async-done | bytes 262160 | tf_op jit(solution)/shard_map/psum | solution.py:103
  1850.7 1.7 copy.71
  (106 shorter events, 7.7 us)
Async XLA Ops:
  7.2 397.6 %copy-start = (f32[512,256]{1,0:T(8,128)S(1)}, f32[512,256]{1,0:T(8,128)}, u32[]{:S(2)}) copy-start(f32[512,256]{1,0:T(8,128)} %param.23) | copy-start | bytes 1572868
  7.2 116.4 %all-reduce.15.cloned.1.call-start = ((), (), s32[]{:S(2)}) async-start(), calls=%async_computation.3 | async-start | bytes 524288 | tf_op jit(solution)/shard_map/psum | solution.py:26
  9.4 186.5 %reduce-scatter.4.cloned.1.call-start = ((), (), s32[]{:S(2)}) async-start(), calls=%async_computation.4 | async-start | bytes 4456448 | tf_op jit(solution)/shard_map/reduce_scatter | solution.py:65
  127.3 1.9 copy-start.1
  131.9 160.4 %copy-start.8 = (f32[128,512]{1,0:T(8,128)S(1)}, f32[128,512]{1,0:T(8,128)}, u32[]{:S(2)}) copy-start(f32[128,512]{1,0:T(8,128)} %param.20) | copy-start | bytes 786436
  131.9 162.4 %copy-start.18 = (s32[4,2]{0,1:T(2,128)S(1)}, s32[4,2]{0,1:T(2,128)}, u32[]{:S(2)}) copy-start(s32[4,2]{0,1:T(2,128)} %param.26) | copy-start | bytes 100
  132.0 160.3 %all-reduce.17.cloned.1.call-start = ((), (), s32[]{:S(2)}) async-start(), calls=%async_computation.5 | async-start | bytes 524288 | tf_op jit(solution)/shard_map/psum | solution.py:66
  195.9 208.9 %all-reduce.19.cloned.1.call-start = ((), (), s32[]{:S(2)}) async-start(), calls=%async_computation.6 | async-start | bytes 524288 | tf_op jit(solution)/shard_map/psum | solution.py:26
  294.3 177.6 %reduce-scatter.6.cloned.1.call-start = ((), (), s32[]{:S(2)}) async-start(), calls=%async_computation.21 | async-start | bytes 2228224 | tf_op jit(solution)/shard_map/reduce_scatter | solution.py:65
  407.9 1.7 copy-start.2
  411.3 60.8 %copy-start.19 = (s32[2,1]{0,1:T(1,128)S(1)}, s32[2,1]{0,1:T(1,128)}, u32[]{:S(2)}) copy-start(s32[2,1]{0,1:T(1,128)} %param.25) | copy-start | bytes 28
  411.3 155.1 %copy-start.10 = (f32[128,256]{1,0:T(8,128)S(1)}, f32[128,256]{1,0:T(8,128)}, u32[]{:S(2)}) copy-start(f32[128,256]{1,0:T(8,128)} %param.19) | copy-start | bytes 393220
  411.3 155.1 %copy-start.17 = (f32[2,128,128]{2,1,0:T(8,128)S(1)}, f32[2,128,128]{2,1,0:T(8,128)}, u32[]{:S(2)}) copy-start(f32[2,128,128]{2,1,0:T(8,128)} %param.15) | copy-start | bytes 393220
  411.3 155.1 %all-reduce.39.cloned.1.call-start = ((), (), s32[]{:S(2)}) async-start(), calls=%async_computation.19 | async-start | bytes 262144 | tf_op jit(solution)/shard_map/psum | solution.py:66
  472.0 206.5 %all-reduce.21.cloned.1.call-start = ((), (), s32[]{:S(2)}) async-start(), calls=%async_computation.7 | async-start | bytes 262144 | tf_op jit(solution)/shard_map/psum | solution.py:26
  568.2 174.4 %reduce-scatter.8.cloned.1.call-start = ((), (), s32[]{:S(2)}) async-start(), calls=%async_computation.22 | async-start | bytes 2228224 | tf_op jit(solution)/shard_map/reduce_scatter | solution.py:65
  571.0 107.5 %copy-start.12 = (f32[256,128]{1,0:T(8,128)S(1)}, f32[256,128]{1,0:T(8,128)}, u32[]{:S(2)}) copy-start(f32[256,128]{1,0:T(8,128)} %param.22) | copy-start | bytes 393220
  681.6 155.3 %copy-start.7 = (f32[256,256]{1,0:T(8,128)S(1)}, f32[256,256]{1,0:T(8,128)}, u32[]{:S(2)}) copy-start(f32[256,256]{1,0:T(8,128)} %param.18) | copy-start | bytes 786436
  681.6 155.3 %copy-start.16 = (f32[1,256,128]{2,1,0:T(8,128)S(1)}, f32[1,256,128]{2,1,0:T(8,128)}, u32[]{:S(2)}) copy-start(f32[1,256,128]{2,1,0:T(8,128)} %param.14) | copy-start | bytes 393220
  681.7 155.3 %all-reduce.41.cloned.1.call-start = ((), (), s32[]{:S(2)}) async-start(), calls=%async_computation.20 | async-start | bytes 262144 | tf_op jit(solution)/shard_map/psum | solution.py:66
  742.6 206.3 %all-reduce.23.cloned.1.call-start = ((), (), s32[]{:S(2)}) async-start(), calls=%async_computation.8 | async-start | bytes 262144 | tf_op jit(solution)/shard_map/psum | solution.py:26
  838.9 207.2 %all-reduce.25.cloned.1.call-start = ((), (), s32[]{:S(2)}) async-start(), calls=%async_computation.9 | async-start | bytes 262144 | tf_op jit(solution)/shard_map/psum | solution.py:103
  950.9 136.2 %all-gather.4.cloned.1.call-start = ((), (), s32[]{:S(2)}) async-start(), calls=%async_computation.10 | async-start | bytes 2228224 | tf_op jit(solution)/shard_map/all_gather | solution.py:166
  1046.2 155.4 %all-reduce.27.cloned.1.call-start = ((), (), s32[]{:S(2)}) async-start(), calls=%async_computation.11 | async-start | bytes 262144 | tf_op jit(solution)/shard_map/psum | solution.py:92
  1091.2 110.4 %copy-start.11 = (f32[1,256,128]{1,2,0:T(8,128)S(1)}, f32[1,256,128]{1,2,0:T(8,128)}, u32[]{:S(2)}) copy-start(f32[1,256,128]{1,2,0:T(8,128)} %all-reduce.21.cloned.1.call-done) | copy-start | bytes 393220
  1093.7 205.0 %all-reduce.29.cloned.1.call-start = ((), (), s32[]{:S(2)}) async-start(), calls=%async_computation.12 | async-start | bytes 262144 | tf_op jit(solution)/shard_map/psum | solution.py:103
  1203.7 136.0 %all-gather.6.cloned.1.call-start = ((), (), s32[]{:S(2)}) async-start(), calls=%async_computation.13 | async-start | bytes 2228224 | tf_op jit(solution)/shard_map/all_gather | solution.py:166
  1298.7 172.2 %all-reduce.31.cloned.1.call-start = ((), (), s32[]{:S(2)}) async-start(), calls=%async_computation.14 | async-start | bytes 524288 | tf_op jit(solution)/shard_map/psum | solution.py:92
  1358.1 112.8 %copy-start.6 = (f32[1,512,128]{1,2,0:T(8,128)S(1)}, f32[1,512,128]{1,2,0:T(8,128)}, u32[]{:S(2)}) copy-start(f32[1,512,128]{1,2,0:T(8,128)} %all-reduce.19.cloned.1.call-done) | copy-start | bytes 786436
  1362.6 207.1 %all-reduce.33.cloned.1.call-start = ((), (), s32[]{:S(2)}) async-start(), calls=%async_computation.15 | async-start | bytes 524288 | tf_op jit(solution)/shard_map/psum | solution.py:103
  1473.2 140.0 %all-gather.8.cloned.1.call-start = ((), (), s32[]{:S(2)}) async-start(), calls=%async_computation.16 | async-start | bytes 4456448 | tf_op jit(solution)/shard_map/all_gather | solution.py:166
  1569.7 180.7 %all-reduce.35.cloned.1.call-start = ((), (), s32[]{:S(2)}) async-start(), calls=%async_computation.17 | async-start | bytes 524288 | tf_op jit(solution)/shard_map/psum | solution.py:92
  1622.7 3.8 copy-start.3
  1636.6 3.8 copy-start.4
  1636.6 113.9 %copy-start.5 = (f32[1,512,128]{1,2,0:T(8,128)S(1)}, f32[1,512,128]{1,2,0:T(8,128)}, u32[]{:S(2)}) copy-start(f32[1,512,128]{1,2,0:T(8,128)} %all-reduce.15.cloned.1.call-done) | copy-start | bytes 786436
  1636.6 113.9 %copy-start.15 = (f32[64,512]{1,0:T(8,128)S(1)}, f32[64,512]{1,0:T(8,128)}, u32[]{:S(2)}) copy-start(f32[64,512]{1,0:T(8,128)} %param.21) | copy-start | bytes 393220
  1640.3 112.3 %copy-start.13 = (f32[1,256,128]{1,2,0:T(8,128)S(1)}, f32[1,256,128]{1,2,0:T(8,128)}, u32[]{:S(2)}) copy-start(f32[1,256,128]{1,2,0:T(8,128)} %all-reduce.25.cloned.1.call-done) | copy-start | bytes 393220
  1640.3 209.0 %copy-start.14 = (f32[2,128,128]{2,1,0:T(8,128)S(1)}, f32[2,128,128]{2,1,0:T(8,128)}, u32[]{:S(2)}) copy-start(f32[2,128,128]{2,1,0:T(8,128)} %all-reduce.29.cloned.1.call-done) | copy-start | bytes 393220
  1640.3 209.6 %copy-start.9 = (f32[4,128,128]{2,1,0:T(8,128)S(1)}, f32[4,128,128]{2,1,0:T(8,128)}, u32[]{:S(2)}) copy-start(f32[4,128,128]{2,1,0:T(8,128)} %all-reduce.33.cloned.1.call-done) | copy-start | bytes 786436
  1641.8 207.5 %all-reduce.37.cloned.1.call-start = ((), (), s32[]{:S(2)}) async-start(), calls=%async_computation.18 | async-start | bytes 524288 | tf_op jit(solution)/shard_map/psum | solution.py:103
Sparse Core Ops, SparseCore 0:
  10.9 112.7 all-reduce.14
  132.1 63.7 reduce-scatter.3
  199.0 93.1 all-reduce.16
  295.0 109.7 all-reduce.18
  411.4 60.4 reduce-scatter.5
  475.0 91.3 all-reduce.38
  569.3 109.2 all-reduce.20
  681.8 60.7 reduce-scatter.7
  745.8 91.1 all-reduce.40
  839.7 109.1 all-reduce.22
  952.7 93.4 all-reduce.24
  1047.9 39.2 all-gather.3
  1093.8 107.7 all-reduce.26
  1205.2 93.4 all-reduce.28
  1300.4 39.2 all-gather.5
  1362.7 108.1 all-reduce.30
  1474.5 95.1 all-reduce.32
  1571.4 41.6 all-gather.7
  1641.9 108.4 all-reduce.34
  1754.1 95.1 all-reduce.36
where the time goes:
time: 1870 us; the launch traced here: 1860 us
  waiting for transfers between devices  1730 us (93%)
  matrix products  56.9 us (3%)
  local copies, waits for them, and re-layouts  35.2 us (2%)
  other arithmetic  18.7 us (1%)
    psum x4, waiting for transfers between devices, forward_solve(): return lax.psum(partial_y, 'rows')  439 us
    psum x4, waiting for transfers between devices, backward_solve(): return lax.psum(dense, 'leaf')  383 us
    psum x3, waiting for transfers between devices, backward_panel(): return solved_rows - lax.psum(partial_g, 'rows')  325 us
    psum x3, waiting for transfers between devices, reduce_dense(): return lax.psum(column_parts, 'leaf')  284 us
    reduce_scatter x3, waiting for transfers between devices, reduce_dense(): lax.psum_scatter(parts, 'rows', scatter_dimension=1, tiled=True)  185 us
    all_gather x3, waiting for transfers between devices, body(): gathered.append(lax.all_gather(solution_cols, 'rows', axis=1, tiled=True))  116 us
  transfers between devices with their start and end apart: 20, of which 20 were waited for; matrix products, arithmetic and copies ran while one was open for 1% of the time, Pallas kernels for 0%

commit v1 on v0

--- a/solution.py
+++ b/solution.py
@@ -163,7 +163,14 @@
         )
         results.append(solution_cols)
         if level_at < 3:
-            gathered.append(lax.all_gather(solution_cols, "rows", axis=1, tiled=True))
+            gathered.append(
+                jnp.concatenate(
+                    lax.all_to_all(
+                        jnp.stack([solution_cols] * lax.axis_size("rows")), "rows", 0, 0
+                    ),
+                    axis=1,
+                )
+            )
     return (results[0], results[1], results[2], results[3])
 
 

time: 1870 us -> 1940 us (1.037)
  blocking collectives: 0 us -> 113 us
  waiting for transfers between devices: 1730 us -> 1700 us
    all_gather x3 -> x0, waiting for transfers between devices: 116 us -> none  [body(): gathered.append(lax.all_gather(solution_cols, 'rows', axis=1, tiled=True))]
    all_to_all x0 -> x2, blocking collectives: none -> 113 us  [body(): lax.all_to_all(jnp.stack([solution_cols] * lax.axis_size('rows')), 'rows'...]
    all_to_all x0 -> x1, waiting for transfers between devices: none -> 83.2 us  [body(): lax.all_to_all(jnp.stack([solution_cols] * lax.axis_size('rows')), 'rows'...]
  transfers between devices with their start and end apart: 20 -> 18, of which waited for: 20 -> 18; matrix products, arithmetic and copies ran while one was open for 1% -> 1% of each run, Pallas kernels for 0% -> 0%
where the time goes in v1:
time: 1940 us; the launch traced here: 1930 us
  waiting for transfers between devices  1700 us (88%)
  blocking collectives  113 us (6%)
  matrix products  66.9 us (3%)
  local copies, waits for them, and re-layouts  20.3 us (1%)
    psum x4, waiting for transfers between devices, forward_solve(): return lax.psum(partial_y, 'rows')  439 us
    psum x4, waiting for transfers between devices, backward_solve(): return lax.psum(dense, 'leaf')  383 us
    psum x3, waiting for transfers between devices, backward_panel(): return solved_rows - lax.psum(partial_g, 'rows')  321 us
    psum x3, waiting for transfers between devices, reduce_dense(): return lax.psum(column_parts, 'leaf')  284 us
    reduce_scatter x3, waiting for transfers between devices, reduce_dense(): lax.psum_scatter(parts, 'rows', scatter_dimension=1, tiled=True)  185 us
    all_to_all x2, blocking collectives, body(): lax.all_to_all(jnp.stack([solution_cols] * lax.axis_size('rows')), 'rows'...  113 us
    all_to_all x1, waiting for transfers between devices, body(): lax.all_to_all(jnp.stack([solution_cols] * lax.axis_size('rows')), 'rows'...  83.2 us
  transfers between devices with their start and end apart: 18, of which 18 were waited for; matrix products, arithmetic and copies ran while one was open for 1% of the time, Pallas kernels for 0%

profile of v1, /device:TPU:2, one launch (start us, length us, event | category | flops | bytes accessed | tf_op | source)
XLA Modules:
  0.0 1933.9 jit_solution(9216670409224538653)
XLA Ops:
  7.2 2.1 convolution_bitcast_fusion.5
  9.4 0.9 fusion.48
  10.3 113.3 %all-reduce.15.cloned.1.call-done = f32[1,512,128]{1,2,0:T(8,128)} async-done(((f32[1,512,128]{1,2,0:T(8,128)}), f32[1,512,128]{1,2,0:T(8,128)}) %all-reduce.15.cloned.1.call-update) | async-done | bytes 262160 | tf_op jit(solution)/shard_map/psum | solution.py:26
  123.6 1.5 convolution_bitcast_fusion.8
  125.4 1.9 convolution_bitcast_fusion
  127.5 1.8 copy-done.1
  129.6 2.3 broadcast_multiply_fusion
  132.0 63.9 %reduce-scatter.4.cloned.1.call-done = f32[4,128,128]{2,1,0:T(8,128)} async-done(((f32[4,2048,128]{2,1,0:T(8,128)}), f32[4,128,128]{2,1,0:T(8,128)}) %reduce-scatter.4.cloned.1.call-update) | async-done | bytes 262160 | tf_op jit(solution)/shard_map/reduce_scatter | solution.py:65
  196.0 96.3 %all-reduce.17.cloned.1.call-done = f32[4,128,128]{2,1,0:T(8,128)} async-done(((f32[4,128,128]{2,1,0:T(8,128)}), f32[4,128,128]{2,1,0:T(8,128)}) %all-reduce.17.cloned.1.call-update) | async-done | bytes 262160 | tf_op jit(solution)/shard_map/psum | solution.py:66
  292.3 2.0 convolution_bitcast_fusion.4
  294.9 109.9 %all-reduce.19.cloned.1.call-done = f32[1,512,128]{1,2,0:T(8,128)} async-done(((f32[1,512,128]{1,2,0:T(8,128)}), f32[1,512,128]{1,2,0:T(8,128)}) %all-reduce.19.cloned.1.call-update) | async-done | bytes 262160 | tf_op jit(solution)/shard_map/psum | solution.py:26
  404.8 1.3 convolution_bitcast_fusion.7
  406.3 1.5 convolution_bitcast_fusion.1
  408.3 1.3 copy-done.2
  409.6 1.7 multiply_add_fusion
  411.4 60.8 %reduce-scatter.6.cloned.1.call-done = f32[2,128,128]{2,1,0:T(8,128)} async-done(((f32[2,2048,128]{2,1,0:T(8,128)}), f32[2,128,128]{2,1,0:T(8,128)}) %reduce-scatter.6.cloned.1.call-update) | async-done | bytes 131088 | tf_op jit(solution)/shard_map/reduce_scatter | solution.py:65
  472.8 0.6 compare_convert_fusion.3
  473.5 93.1 %all-reduce.39.cloned.1.call-done = f32[2,128,128]{2,1,0:T(8,128)} async-done(((f32[2,128,128]{2,1,0:T(8,128)}), f32[2,128,128]{2,1,0:T(8,128)}) %all-reduce.39.cloned.1.call-update) | async-done | bytes 131088 | tf_op jit(solution)/shard_map/psum | solution.py:66
  566.6 1.8 convolution_bitcast_fusion.10
  568.5 2.8 fusion.6
  571.3 1.2 copy.43
  572.5 106.2 %all-reduce.21.cloned.1.call-done = f32[1,256,128]{1,2,0:T(8,128)} async-done(((f32[1,256,128]{1,2,0:T(8,128)}), f32[1,256,128]{1,2,0:T(8,128)}) %all-reduce.21.cloned.1.call-update) | async-done | bytes 131088 | tf_op jit(solution)/shard_map/psum | solution.py:26
  678.7 1.2 convolution_bitcast_fusion.12
  680.2 1.6 bitcast_add_fusion
  681.9 60.9 %reduce-scatter.8.cloned.1.call-done = f32[1,256,128]{2,1,0:T(8,128)} async-done(((f32[1,4096,128]{2,1,0:T(8,128)}), f32[1,256,128]{2,1,0:T(8,128)}) %reduce-scatter.8.cloned.1.call-update) | async-done | bytes 131088 | tf_op jit(solution)/shard_map/reduce_scatter | solution.py:65
  742.9 94.6 %all-reduce.41.cloned.1.call-done = f32[1,256,128]{2,1,0:T(8,128)} async-done(((f32[1,256,128]{2,1,0:T(8,128)}), f32[1,256,128]{2,1,0:T(8,128)}) %all-reduce.41.cloned.1.call-update) | async-done | bytes 131088 | tf_op jit(solution)/shard_map/psum | solution.py:66
  837.4 2.0 convolution_bitcast_fusion.6
  839.5 109.9 %all-reduce.23.cloned.1.call-done = f32[256,128]{0,1:T(8,128)} async-done(((f32[256,128]{0,1:T(8,128)}), f32[256,128]{0,1:T(8,128)}) %all-reduce.23.cloned.1.call-update) | async-done | bytes 131088 | tf_op jit(solution)/shard_map/psum | solution.py:26
  949.4 2.0 fusion.13
  951.4 95.2 %all-reduce.25.cloned.1.call-done = f32[1,256,128]{1,2,0:T(8,128)} async-done(((f32[1,256,128]{1,2,0:T(8,128)}), f32[1,256,128]{1,2,0:T(8,128)}) %all-reduce.25.cloned.1.call-update) | async-done | bytes 131088 | tf_op jit(solution)/shard_map/psum | solution.py:103
  1046.6 1.0 copy.47
  1047.8 56.7 %all_to_all.15 = f32[16,1,256,128]{3,2,1,0:T(8,128)S(1)} all-to-all(f32[16,1,256,128]{3,2,1,0:T(8,128)S(1)} %stack.6), channel_id=1, replica_groups=mesh['leaf'=16,'rows'=16] {'rows'}, dimensions={0} | all-to-all | bytes 4194304 | tf_op jit(solution)/shard_map/all_to_all | solution.py:168
  1104.5 2.1 broadcast_multiply_fusion.1
  1106.7 2.6 fusion.7
  1109.3 1.0 convolution_bitcast_fusion.9
  1110.4 106.6 %all-reduce.27.cloned.1.call-done = f32[1,256,128]{1,2,0:T(8,128)} async-done(((f32[1,256,128]{1,2,0:T(8,128)}), f32[1,256,128]{1,2,0:T(8,128)}) %all-reduce.27.cloned.1.call-update) | async-done | bytes 131088 | tf_op jit(solution)/shard_map/psum | solution.py:92
  1216.9 1.2 convolution_bitcast_fusion.11
  1218.2 0.7 broadcast_multiply_fusion.6
  1219.0 95.1 %all-reduce.29.cloned.1.call-done = f32[2,128,128]{2,1,0:T(8,128)} async-done(((f32[2,128,128]{2,1,0:T(8,128)}), f32[2,128,128]{2,1,0:T(8,128)}) %all-reduce.29.cloned.1.call-update) | async-done | bytes 131088 | tf_op jit(solution)/shard_map/psum | solution.py:103
  1314.2 1.1 stack.7
  1315.3 56.6 %all_to_all.16 = f32[16,2,128,128]{3,2,1,0:T(8,128)S(1)} all-to-all(f32[16,2,128,128]{3,2,1,0:T(8,128)S(1)} %stack.7), channel_id=1, replica_groups=mesh['leaf'=16,'rows'=16] {'rows'}, dimensions={0} | all-to-all | bytes 4194304 | tf_op jit(solution)/shard_map/all_to_all | solution.py:168
  1372.1 10.1 fusion.11
  1382.5 3.0 fusion.4
  1385.4 1.4 convolution_bitcast_fusion.3
  1386.9 106.9 %all-reduce.31.cloned.1.call-done = f32[1,512,128]{1,2,0:T(8,128)} async-done(((f32[1,512,128]{1,2,0:T(8,128)}), f32[1,512,128]{1,2,0:T(8,128)}) %all-reduce.31.cloned.1.call-update) | async-done | bytes 262160 | tf_op jit(solution)/shard_map/psum | solution.py:92
  1493.9 1.3 convolution_bitcast_fusion.13
  1495.3 0.8 broadcast_multiply_fusion.5
  1496.1 96.6 %all-reduce.33.cloned.1.call-done = f32[4,128,128]{2,1,0:T(8,128)} async-done(((f32[4,128,128]{2,1,0:T(8,128)}), f32[4,128,128]{2,1,0:T(8,128)}) %all-reduce.33.cloned.1.call-update) | async-done | bytes 262160 | tf_op jit(solution)/shard_map/psum | solution.py:103
  1592.7 3.4 stack.8
  1596.1 7.3 all-to-all-start.2
  1603.7 10.9 fusion.9
  1614.6 83.2 %all-to-all-done.2 = f32[16,4,128,128]{3,2,1,0:T(8,128)} async-done(((f32[16,4,128,128]{3,2,1,0:T(8,128)}), f32[16,4,128,128]{3,2,1,0:T(8,128)}, u32[]{:S(2)}, u32[]{:S(2)}) %all-to-all-start.2) | async-done | bytes 4194336 | tf_op jit(solution)/shard_map/all_to_all | solution.py:168
  1697.8 2.7 copy.53
  1700.5 11.4 fusion
  1712.3 3.9 fusion.2
  1716.2 1.4 convolution_bitcast_fusion.2
  1717.7 107.3 %all-reduce.35.cloned.1.call-done = f32[1,512,128]{1,2,0:T(8,128)} async-done(((f32[1,512,128]{1,2,0:T(8,128)}), f32[1,512,128]{1,2,0:T(8,128)}) %all-reduce.35.cloned.1.call-update) | async-done | bytes 262160 | tf_op jit(solution)/shard_map/psum | solution.py:92
  1825.1 1.3 convolution_bitcast_fusion.14
  1826.4 0.8 broadcast_multiply_fusion.4
  1827.2 0.8 copy.56
  1828.0 95.9 %all-reduce.37.cloned.1.call-done = f32[8,64,128]{2,1,0:T(8,128)} async-done(((f32[8,64,128]{2,1,0:T(8,128)}), f32[8,64,128]{2,1,0:T(8,128)}) %all-reduce.37.cloned.1.call-update) | async-done | bytes 262160 | tf_op jit(solution)/shard_map/psum | solution.py:103
  1923.9 0.7 copy.90
  1924.5 0.7 copy.91
  1925.2 1.7 copy.92
  (105 shorter events, 5.1 us)
Async XLA Ops:
  7.2 397.6 %copy-start = (f32[512,256]{1,0:T(8,128)S(1)}, f32[512,256]{1,0:T(8,128)}, u32[]{:S(2)}) copy-start(f32[512,256]{1,0:T(8,128)} %param.23) | copy-start | bytes 1572868
  7.2 116.4 %all-reduce.15.cloned.1.call-start = ((), (), s32[]{:S(2)}) async-start(), calls=%async_computation.6 | async-start | bytes 524288 | tf_op jit(solution)/shard_map/psum | solution.py:26
  9.4 186.5 %reduce-scatter.4.cloned.1.call-start = ((), (), s32[]{:S(2)}) async-start(), calls=%async_computation.7 | async-start | bytes 4456448 | tf_op jit(solution)/shard_map/reduce_scatter | solution.py:65
  127.3 1.9 copy-start.1
  131.9 160.4 %copy-start.11 = (f32[128,512]{1,0:T(8,128)S(1)}, f32[128,512]{1,0:T(8,128)}, u32[]{:S(2)}) copy-start(f32[128,512]{1,0:T(8,128)} %param.20) | copy-start | bytes 786436
  131.9 162.4 %copy-start.21 = (s32[4,2]{0,1:T(2,128)S(1)}, s32[4,2]{0,1:T(2,128)}, u32[]{:S(2)}) copy-start(s32[4,2]{0,1:T(2,128)} %param.26) | copy-start | bytes 100
  131.9 160.3 %all-reduce.17.cloned.1.call-start = ((), (), s32[]{:S(2)}) async-start(), calls=%async_computation.8 | async-start | bytes 524288 | tf_op jit(solution)/shard_map/psum | solution.py:66
  195.9 208.9 %all-reduce.19.cloned.1.call-start = ((), (), s32[]{:S(2)}) async-start(), calls=%async_computation.9 | async-start | bytes 524288 | tf_op jit(solution)/shard_map/psum | solution.py:26
  294.3 177.8 %reduce-scatter.6.cloned.1.call-start = ((), (), s32[]{:S(2)}) async-start(), calls=%async_computation.21 | async-start | bytes 2228224 | tf_op jit(solution)/shard_map/reduce_scatter | solution.py:65
  407.9 1.7 copy-start.2
  411.3 61.0 %copy-start.22 = (s32[2,1]{0,1:T(1,128)S(1)}, s32[2,1]{0,1:T(1,128)}, u32[]{:S(2)}) copy-start(s32[2,1]{0,1:T(1,128)} %param.25) | copy-start | bytes 28
  411.3 155.3 %copy-start.13 = (f32[128,256]{1,0:T(8,128)S(1)}, f32[128,256]{1,0:T(8,128)}, u32[]{:S(2)}) copy-start(f32[128,256]{1,0:T(8,128)} %param.19) | copy-start | bytes 393220
  411.3 155.3 %copy-start.20 = (f32[2,128,128]{2,1,0:T(8,128)S(1)}, f32[2,128,128]{2,1,0:T(8,128)}, u32[]{:S(2)}) copy-start(f32[2,128,128]{2,1,0:T(8,128)} %param.15) | copy-start | bytes 393220
  411.3 155.3 %all-reduce.39.cloned.1.call-start = ((), (), s32[]{:S(2)}) async-start(), calls=%async_computation.19 | async-start | bytes 262144 | tf_op jit(solution)/shard_map/psum | solution.py:66
  472.2 206.6 %all-reduce.21.cloned.1.call-start = ((), (), s32[]{:S(2)}) async-start(), calls=%async_computation.10 | async-start | bytes 262144 | tf_op jit(solution)/shard_map/psum | solution.py:26
  568.4 174.4 %reduce-scatter.8.cloned.1.call-start = ((), (), s32[]{:S(2)}) async-start(), calls=%async_computation.22 | async-start | bytes 2228224 | tf_op jit(solution)/shard_map/reduce_scatter | solution.py:65
  571.2 107.5 %copy-start.16 = (f32[256,128]{1,0:T(8,128)S(1)}, f32[256,128]{1,0:T(8,128)}, u32[]{:S(2)}) copy-start(f32[256,128]{1,0:T(8,128)} %param.22) | copy-start | bytes 393220
  681.8 155.6 %copy-start.10 = (f32[256,256]{1,0:T(8,128)S(1)}, f32[256,256]{1,0:T(8,128)}, u32[]{:S(2)}) copy-start(f32[256,256]{1,0:T(8,128)} %param.18) | copy-start | bytes 786436
  681.8 155.6 %copy-start.19 = (f32[1,256,128]{2,1,0:T(8,128)S(1)}, f32[1,256,128]{2,1,0:T(8,128)}, u32[]{:S(2)}) copy-start(f32[1,256,128]{2,1,0:T(8,128)} %param.14) | copy-start | bytes 393220
  681.9 155.5 %all-reduce.41.cloned.1.call-start = ((), (), s32[]{:S(2)}) async-start(), calls=%async_computation.20 | async-start | bytes 262144 | tf_op jit(solution)/shard_map/psum | solution.py:66
  742.8 206.6 %all-reduce.23.cloned.1.call-start = ((), (), s32[]{:S(2)}) async-start(), calls=%async_computation.11 | async-start | bytes 262144 | tf_op jit(solution)/shard_map/psum | solution.py:26
  839.4 207.2 %all-reduce.25.cloned.1.call-start = ((), (), s32[]{:S(2)}) async-start(), calls=%async_computation.12 | async-start | bytes 262144 | tf_op jit(solution)/shard_map/psum | solution.py:103
  951.4 265.6 %all-reduce.27.cloned.1.call-start = ((), (), s32[]{:S(2)}) async-start(), calls=%async_computation.13 | async-start | bytes 262144 | tf_op jit(solution)/shard_map/psum | solution.py:92
  1106.7 110.3 %copy-start.14 = (f32[1,256,128]{1,2,0:T(8,128)S(1)}, f32[1,256,128]{1,2,0:T(8,128)}, u32[]{:S(2)}) copy-start(f32[1,256,128]{1,2,0:T(8,128)} %all-reduce.21.cloned.1.call-done) | copy-start | bytes 393220
  1110.3 203.8 %all-reduce.29.cloned.1.call-start = ((), (), s32[]{:S(2)}) async-start(), calls=%async_computation.14 | async-start | bytes 262144 | tf_op jit(solution)/shard_map/psum | solution.py:103
  1219.0 274.9 %all-reduce.31.cloned.1.call-start = ((), (), s32[]{:S(2)}) async-start(), calls=%async_computation.15 | async-start | bytes 524288 | tf_op jit(solution)/shard_map/psum | solution.py:92
  1372.1 10.3 copy-start.5
  1382.4 111.4 %copy-start.8 = (f32[1,512,128]{1,2,0:T(8,128)S(1)}, f32[1,512,128]{1,2,0:T(8,128)}, u32[]{:S(2)}) copy-start(f32[1,512,128]{1,2,0:T(8,128)} %all-reduce.19.cloned.1.call-done) | copy-start | bytes 786436
  1386.9 205.8 %all-reduce.33.cloned.1.call-start = ((), (), s32[]{:S(2)}) async-start(), calls=%async_computation.16 | async-start | bytes 524288 | tf_op jit(solution)/shard_map/psum | solution.py:103
  1596.1 7.6 copy-start.6
  1596.1 101.6 %all-to-all-start.2 = ((f32[16,4,128,128]{3,2,1,0:T(8,128)}), f32[16,4,128,128]{3,2,1,0:T(8,128)}, u32[]{:S(2)}, u32[]{:S(2)}) async-start(f32[16,4,128,128]{3,2,1,0:T(8,128)} %stack.8), calls=%async_computation.3 | async-start | bytes 8388608 | tf_op jit(solution)/shard_map/all_to_all | solution.py:168
  1603.4 221.6 %all-reduce.35.cloned.1.call-start = ((), (), s32[]{:S(2)}) async-start(), calls=%async_computation.17 | async-start | bytes 524288 | tf_op jit(solution)/shard_map/psum | solution.py:92
  1700.5 11.5 copy-start.3
  1700.5 11.5 copy-start.12
  1712.2 4.0 copy-start.4
  1712.2 112.8 %copy-start.7 = (f32[1,512,128]{1,2,0:T(8,128)S(1)}, f32[1,512,128]{1,2,0:T(8,128)}, u32[]{:S(2)}) copy-start(f32[1,512,128]{1,2,0:T(8,128)} %all-reduce.15.cloned.1.call-done) | copy-start | bytes 786436
  1712.3 112.8 %copy-start.18 = (f32[64,512]{1,0:T(8,128)S(1)}, f32[64,512]{1,0:T(8,128)}, u32[]{:S(2)}) copy-start(f32[64,512]{1,0:T(8,128)} %param.21) | copy-start | bytes 393220
  1716.2 111.1 %copy-start.17 = (f32[1,256,128]{1,2,0:T(8,128)S(1)}, f32[1,256,128]{1,2,0:T(8,128)}, u32[]{:S(2)}) copy-start(f32[1,256,128]{1,2,0:T(8,128)} %all-reduce.25.cloned.1.call-done) | copy-start | bytes 393220
  1716.2 207.7 %copy-start.15 = (f32[2,128,128]{2,1,0:T(8,128)S(1)}, f32[2,128,128]{2,1,0:T(8,128)}, u32[]{:S(2)}) copy-start(f32[2,128,128]{2,1,0:T(8,128)} %all-reduce.29.cloned.1.call-done) | copy-start | bytes 393220
  1716.2 208.4 %copy-start.9 = (f32[4,128,128]{2,1,0:T(8,128)S(1)}, f32[4,128,128]{2,1,0:T(8,128)}, u32[]{:S(2)}) copy-start(f32[4,128,128]{2,1,0:T(8,128)} %all-reduce.33.cloned.1.call-done) | copy-start | bytes 786436
  1717.7 206.2 %all-reduce.37.cloned.1.call-start = ((), (), s32[]{:S(2)}) async-start(), calls=%async_computation.18 | async-start | bytes 524288 | tf_op jit(solution)/shard_map/psum | solution.py:103
Sparse Core Ops, SparseCore 0:
  10.9 112.7 all-reduce.14
  132.1 63.7 reduce-scatter.3
  199.0 93.1 all-reduce.16
  295.0 109.7 all-reduce.18
  411.4 60.6 reduce-scatter.5
  475.2 91.3 all-reduce.38
  569.5 109.2 all-reduce.20
  682.0 60.7 reduce-scatter.7
  746.0 91.3 all-reduce.40
  840.1 109.1 all-reduce.22
  953.2 93.4 all-reduce.24
  1110.4 106.4 all-reduce.26
  1220.7 93.4 all-reduce.28
  1387.0 106.8 all-reduce.30
  1497.5 95.1 all-reduce.32
  1717.8 107.2 all-reduce.34
  1828.7 95.1 all-reduce.36
